TPU v7x, 128 devices: a whole 4x4x4 slice. The times are simulated.
128 devices in a mesh: sec: 4 (over y_hi, core), dev: 32 (over z, y_lo, x).
Axes of the slice: x: 4, y: 4 (y_hi: 2, y_lo: 2; y = y_hi * 2 + y_lo), z: 4, core: 2. Of those that a mesh axis runs over, the one named last changes fastest.
Arguments:
- queries: bfloat16 [256, 8192], P('dev', 'sec')
- fresh_key_value: bfloat16 [2, 256, 512], P(None, 'dev', 'sec'), may hold values from -6 to 6
- key_value_cache: bfloat16 [2, 256, 1024, 512], P(None, 'dev', None, 'sec'), may hold values from -6 to 6
- lengths: int32 [256], P('dev'), may hold values from 1 to 1024, as said below
- residual: bfloat16 [256, 4096], P(None, 'dev'), may hold values from -6 to 6
- out_weight: bfloat16 [8192, 4096], P('sec', 'dev'), may hold values from -0.0625 to 0.0625
- norm_gain: float32 [4096], P('dev'), may hold values from 0.1 to 1.9
- routes: int32 [256, 8], replicated, may hold values from 0 to 63, all different within a row; in each aligned block of 256 rows (0 to 255, 256 to 511, ...) at most 64 rows name the same one
- route_weights: float32 [256, 8], replicated, may hold values from 0.05 to 0.5
- w_gate: bfloat16 [64, 4096, 1536], P('dev', None, 'sec'), may hold values from -0.09375 to 0.09375
- w_up: bfloat16 [64, 4096, 1536], P('dev', None, 'sec'), may hold values from -0.09375 to 0.09375
- w_down: bfloat16 [64, 1536, 4096], P('dev', 'sec'), may hold values from -0.15625 to 0.15625
Outputs:
- layer_out: bfloat16 [256, 4096], P(None, 'dev')
Inputs may be any that keep to these rules, and one draw needn't show every extreme that they name: `routes`: each row names 8 different experts; no expert is named by more than 64 rows, a bound that some block reaches. `lengths`: some row has all 1024 slots filled.
All inputs are finite; a program needn't handle non-finite values.
Results may differ from a plain program's by a relative error of at most 0.0055.
Values may be sent and summed in bfloat16 or wider, within the bound.
No kernel may reach another device: no remote copies, remote signals or barrier semaphores. Data moves between devices by JAX's collectives and lax.ppermute only.
A program may use at most 128 MiB of HBM per device.

v0:
```python
import math
import jax
import jax.numpy as jnp
from jax import lax
from jax.sharding import PartitionSpec as P

D = 4096
QUERY_HEADS = 64
KEY_VALUE_HEADS = 4
HEAD_SIZE = 128
CAP = 64


def attend(queries, fresh_key_value, key_value_cache, lengths):
    row_count = key_value_cache.shape[1]
    cache_length = key_value_cache.shape[2]
    heads_kv = key_value_cache.shape[3] // HEAD_SIZE
    queries_per_group = QUERY_HEADS // KEY_VALUE_HEADS
    score_scale = 1.0 / math.sqrt(HEAD_SIZE)
    head_queries = queries.reshape(row_count, heads_kv, queries_per_group, HEAD_SIZE)
    cached_keys = key_value_cache[0].reshape(row_count, cache_length, heads_kv, HEAD_SIZE)
    cached_values = key_value_cache[1].reshape(row_count, cache_length, heads_kv, HEAD_SIZE)
    own_key = fresh_key_value[0].reshape(row_count, heads_kv, HEAD_SIZE)
    own_value = fresh_key_value[1].reshape(row_count, heads_kv, HEAD_SIZE).astype(jnp.float32)
    scores = (
        jnp.einsum("rkgd,rtkd->rkgt", head_queries, cached_keys, preferred_element_type=jnp.float32)
        * score_scale
    )
    own_score = (
        jnp.einsum("rkgd,rkd->rkg", head_queries, own_key, preferred_element_type=jnp.float32)
        * score_scale
    )
    visible = (jnp.arange(cache_length, dtype=jnp.int32)[None, :] < lengths[:, None])[
        :, None, None, :
    ]
    row_max = jnp.maximum(jnp.max(jnp.where(visible, scores, -jnp.inf), axis=-1), own_score)
    weights = jnp.where(visible, jnp.exp(scores - row_max[..., None]), 0.0)
    own_weight = jnp.exp(own_score - row_max)
    normalizer = jnp.sum(weights, axis=-1) + own_weight
    weighted = jnp.einsum(
        "rkgt,rtkd->rkgd",
        weights.astype(jnp.bfloat16),
        cached_values,
        preferred_element_type=jnp.float32,
    )
    weighted = weighted + own_weight[..., None] * own_value[:, :, None, :]
    return (
        (weighted / normalizer[..., None])
        .astype(jnp.bfloat16)
        .reshape(row_count, heads_kv * queries_per_group * HEAD_SIZE)
    )


def slot_layout(routes, route_weights, expert_ids):
    matches = routes[:, :, None] == expert_ids[None, None, :]
    chosen = jnp.any(matches, axis=1)
    shares = jnp.sum(jnp.where(matches, route_weights[:, :, None], 0.0), axis=1)
    slot_rank = jnp.cumsum(chosen.astype(jnp.int32), axis=0, dtype=jnp.int32) - 1
    slot_ids = jnp.arange(CAP, dtype=jnp.int32)
    slot_mask = (chosen[:, :, None] & (slot_rank[:, :, None] == slot_ids[None, None, :])).transpose(
        1, 2, 0
    )
    spread = slot_mask.astype(jnp.float32) * shares.T[:, None, :]
    return (slot_mask, spread)


def expert_results(full_rows, slot_mask, w_gate, w_up, w_down):
    picked = jnp.einsum(
        "ecr,rd->ecd", slot_mask.astype(jnp.bfloat16), full_rows, preferred_element_type=jnp.float32
    ).astype(jnp.bfloat16)
    gate_part = jnp.einsum("ecd,edf->ecf", picked, w_gate, preferred_element_type=jnp.float32)
    upward = jnp.einsum("ecd,edf->ecf", picked, w_up, preferred_element_type=jnp.float32)
    activation = (jax.nn.silu(gate_part) * upward).astype(jnp.bfloat16)
    return jnp.einsum("ecf,efd->ecd", activation, w_down, preferred_element_type=jnp.float32)


def shards(
    queries,
    fresh_key_value,
    key_value_cache,
    lengths,
    residual,
    out_weight,
    norm_gain,
    routes,
    route_weights,
    w_gate,
    w_up,
    w_down,
):
    attn = attend(queries, fresh_key_value, key_value_cache, lengths)
    partial_out = jnp.dot(
        lax.all_gather(attn, "dev", axis=0, tiled=True),
        out_weight,
        preferred_element_type=jnp.float32,
    )
    hidden = residual.astype(jnp.float32) + lax.psum(partial_out, "sec")
    square_sum = lax.psum(jnp.sum(hidden * hidden, axis=-1, keepdims=True), "dev")
    normed = (hidden * lax.rsqrt(square_sum / D + 1e-06) * norm_gain).astype(jnp.bfloat16)
    full_rows = lax.all_gather(normed, "dev", axis=1, tiled=True)
    local_count = w_gate.shape[0]
    local_ids = lax.axis_index("dev") * local_count + jnp.arange(local_count, dtype=jnp.int32)
    slot_mask, spread = slot_layout(routes, route_weights, local_ids)
    result = expert_results(full_rows, slot_mask, w_gate, w_up, w_down)
    expert_term = jnp.einsum("ecr,ecd->rd", spread, result, precision=lax.Precision.HIGHEST)
    mixture = lax.psum(lax.psum_scatter(expert_term, "dev", scatter_dimension=1, tiled=True), "sec")
    return (hidden + mixture).astype(jnp.bfloat16)


def solution(mesh):
    return jax.shard_map(
        shards,
        mesh=mesh,
        in_specs=(
            P("dev", "sec"),
            P(None, "dev", "sec"),
            P(None, "dev", None, "sec"),
            P("dev"),
            P(None, "dev"),
            P("sec", "dev"),
            P("dev"),
            P(),
            P(),
            P("dev", None, "sec"),
            P("dev", None, "sec"),
            P("dev", "sec", None),
        ),
        out_specs=P(None, "dev"),
        check_vma=False,
    )
```

profile of v0, /device:TPU:1, one launch (start us, length us, event | category | flops | bytes accessed | tf_op | source)
XLA Modules:
  0.0 653.0 jit_solution(15178874167412993256)
XLA Ops:
  6.5 0.0 copy-start
  6.5 0.0 copy-start.2
  6.5 0.0 all-gather.3.cloned.1.call-start
  6.5 0.8 bitcast_convert_fusion
  7.3 0.7 iota_compare_fusion.1
  8.0 0.9 fusion.46
  8.9 0.0 copy-start.5
  8.9 0.0 copy-start.3
  8.9 0.0 copy-start.4
  8.9 2.4 select_reduce_fusion
  11.3 0.2 fusion.24
  11.6 2.1 fusion.21
  13.7 0.6 copy.34
  14.3 0.0 all-gather.3.cloned.1.call-update
  14.3 0.0 all-reduce.3.cloned.1.call-start
  14.4 132.9 %all-gather.3.cloned.1.call-done = bf16[256,2048]{1,0:T(8,128)(2,1)} async-done(((bf16[8,2048]{1,0:T(8,128)(2,1)}), bf16[256,2048]{1,0:T(8,128)(2,1)}) %all-gather.3.cloned.1.call-update) | async-done | bytes 1048592 | tf_op jit(solution)/shard_map/all_gather | solution.py:93
  147.2 0.0 copy-done
  147.2 2.3 fusion.55
  149.5 0.0 all-reduce.3.cloned.1.call-update
  149.5 0.0 all-gather.5.cloned.1.call-start
  149.6 62.2 %all-reduce.3.cloned.1.call-done = f32[256,128]{1,0:T(8,128)} async-done(((f32[256,128]{1,0:T(8,128)}), f32[256,128]{1,0:T(8,128)}) %all-reduce.3.cloned.1.call-update) | async-done | bytes 131088 | tf_op jit(solution)/shard_map/psum | solution.py:97
  211.8 0.0 copy-done.2
  211.8 1.0 multiply_reduce_fusion
  212.9 68.0 %psum.22 = f32[256,1]{0,1:T(1,128)S(1)} all-reduce(f32[256,1]{0,1:T(1,128)S(1)} %bitcast.67), channel_id=1, replica_groups=mesh['sec'=4,'dev'=32] {'dev'}, use_global_device_ids=true, to_apply=%region_8.9 | all-reduce | flops 256 | bytes 2048 | tf_op jit(solution)/shard_map/psum | solution.py:98
  280.9 0.0 copy-done.5
  280.9 1.6 multiply_convert_fusion
  282.5 0.0 all-gather.5.cloned.1.call-update
  282.6 0.0 reduce-scatter.2.cloned.1.call-start
  282.6 0.0 copy-done.3
  282.6 0.1 compare_reduce_fusion
  282.7 0.6 reduce-window.6
  283.4 0.2 slice_reduce_fusion
  283.6 0.2 reduce-window.9
  283.7 0.1 add_bitcast_fusion
  283.8 0.0 copy-done.4
  283.8 0.1 fusion.49
  283.9 116.7 %all-gather.5.cloned.1.call-done = bf16[256,4096]{1,0:T(8,128)(2,1)} async-done(((bf16[256,128]{1,0:T(8,128)(2,1)}), bf16[256,4096]{1,0:T(8,128)(2,1)}) %all-gather.5.cloned.1.call-update) | async-done | bytes 2097168 | tf_op jit(solution)/shard_map/all_gather | solution.py:100
  400.6 2.0 convolution_convert_fusion
  402.6 3.8 fusion.56
  406.4 8.1 %fusion.11 = f32[2,64,4096]{2,1,0:T(8,128)} fusion(bf16[2,384,4096]{2,1,0:T(8,128)(2,1)} %param.23, bf16[2,64,4096]{2,1,0:T(8,128)(2,1)S(1)} %convolution_convert_fusion, bf16[2,4096,384]{2,1,0:T(8,128)(2,1)} %param.22, f32[2,64,384]{2,1,0:T(8,128)S(1)} %fusion.56), kind=kOutput, calls=%fused_computation.12 | convolution fusion | flops 805601280 | bytes 15925248 | tf_op jit(solution)/shard_map/ecf,efd->ecd/dot_general | solution.py:74
  414.5 6.8 %convolution_bitcast_fusion = f32[256,4096]{1,0:T(8,128)} fusion(f32[2,64,4096]{2,1,0:T(8,128)} %fusion.11, f32[2,256]{1,0:T(2,128)S(1)} %bitcast.65, s32[2,256]{1,0:T(2,128)S(1)} %bitcast.58, pred[2,256]{1,0:T(4,128)(4,1)S(1)} %bitcast.62), kind=kOutput, calls=%fused_computation | convolution fusion | flops 1610711040 | bytes 6296064 | tf_op jit(solution)/shard_map/ecr,ecd->rd/dot_general | solution.py:105
  421.3 0.0 reduce-scatter.2.cloned.1.call-update
  421.3 0.0 all-reduce.5.cloned.1.call-start
  421.4 162.3 %reduce-scatter.2.cloned.1.call-done = f32[256,128]{1,0:T(8,128)} async-done(((f32[256,4096]{1,0:T(8,128)}), f32[256,128]{1,0:T(8,128)}) %reduce-scatter.2.cloned.1.call-update) | async-done | bytes 131088 | tf_op jit(solution)/shard_map/reduce_scatter | solution.py:106
  583.7 0.0 all-reduce.5.cloned.1.call-update
  583.7 61.2 %all-reduce.5.cloned.1.call-done = f32[256,128]{1,0:T(8,128)} async-done(((f32[256,128]{1,0:T(8,128)}), f32[256,128]{1,0:T(8,128)}) %all-reduce.5.cloned.1.call-update) | async-done | bytes 131088 | tf_op jit(solution)/shard_map/psum | solution.py:106
  645.0 0.0 copy-done.1
  645.0 1.6 add_convert_fusion
  (8 shorter events, 0.1 us)
Async XLA Ops:
  6.5 140.7 %copy-start = (bf16[2048,128]{1,0:T(8,128)(2,1)S(1)}, bf16[2048,128]{1,0:T(8,128)(2,1)}, u32[]{:S(2)}) copy-start(bf16[2048,128]{1,0:T(8,128)(2,1)} %param.17) | copy-start | bytes 1572868
  6.5 205.3 %copy-start.2 = (bf16[256,128]{1,0:T(8,128)(2,1)S(1)}, bf16[256,128]{1,0:T(8,128)(2,1)}, u32[]{:S(2)}) copy-start(bf16[256,128]{1,0:T(8,128)(2,1)} %param.16) | copy-start | bytes 196612
  6.5 140.7 %all-gather.3.cloned.1.call-start = ((), (), s32[]{:S(2)}) async-start(), calls=%async_computation.1 | async-start | bytes 1081344 | tf_op jit(solution)/shard_map/all_gather | solution.py:93
  8.9 272.0 %copy-start.5 = (f32[128]{0:T(128)S(1)}, f32[128]{0:T(128)}, u32[]{:S(2)}) copy-start(f32[128]{0:T(128)} %param.18) | copy-start | bytes 1540
  8.9 273.7 %copy-start.3 = (s32[256,8]{0,1:T(8,128)S(1)}, s32[256,8]{0,1:T(8,128)}, u32[]{:S(2)}) copy-start(s32[256,8]{0,1:T(8,128)} %param.19) | copy-start | bytes 24580
  8.9 274.9 %copy-start.4 = (f32[256,8]{0,1:T(8,128)S(1)}, f32[256,8]{0,1:T(8,128)}, u32[]{:S(2)}) copy-start(f32[256,8]{0,1:T(8,128)} %param.20) | copy-start | bytes 24580
  14.3 197.5 %all-reduce.3.cloned.1.call-start = ((), (), s32[]{:S(2)}) async-start(), calls=%async_computation.2 | async-start | bytes 262144 | tf_op jit(solution)/shard_map/psum | solution.py:97
  149.5 251.0 %all-gather.5.cloned.1.call-start = ((), (), s32[]{:S(2)}) async-start(), calls=%async_computation.3 | async-start | bytes 2162688 | tf_op jit(solution)/shard_map/all_gather | solution.py:100
  282.6 301.2 %reduce-scatter.2.cloned.1.call-start = ((), (), s32[]{:S(2)}) async-start(), calls=%async_computation.4 | async-start | bytes 4325376 | tf_op jit(solution)/shard_map/reduce_scatter | solution.py:106
  414.5 230.4 %copy-start.1 = (f32[256,128]{1,0:T(8,128)S(1)}, f32[256,128]{1,0:T(8,128)}, u32[]{:S(2)}) copy-start(f32[256,128]{1,0:T(8,128)} %all-reduce.3.cloned.1.call-done) | copy-start | bytes 393220
  421.3 223.6 %all-reduce.5.cloned.1.call-start = ((), (), s32[]{:S(2)}) async-start(), calls=%async_computation.5 | async-start | bytes 262144 | tf_op jit(solution)/shard_map/psum | solution.py:106
Sparse Core Ops, SparseCore 0:
  14.4 132.7 all-gather.2
  149.7 62.0 all-reduce.2
  282.7 117.8 all-gather.4
  421.4 162.2 reduce-scatter.1
  586.2 58.7 all-reduce.4
where the time goes:
time: 654 us; the launch traced here: 653 us
  waiting for transfers between devices  535 us (82%)
  blocking collectives  68 us (10%)
  matrix products  28.3 us (4%)
  between operations  13.2 us (2%)
  other arithmetic  7.04 us (1%)
    reduce_scatter x1, waiting for transfers between devices, shards(): lax.psum_scatter(expert_term, 'dev', scatter_dimension=1, tiled=True)  162 us
    all_gather x1, waiting for transfers between devices, shards(): lax.all_gather(attn, 'dev', axis=0, tiled=True)  133 us
    all_gather x1, waiting for transfers between devices, shards(): full_rows = lax.all_gather(normed, 'dev', axis=1, tiled=True)  117 us
    psum x1, blocking collectives, shards(): lax.psum(jnp.sum(hidden * hidden, axis=-1, keepdims=True), 'dev')  68 us
    psum x1, waiting for transfers between devices, shards(): hidden = residual.astype(jnp.float32) + lax.psum(partial_out, 'sec')  62.2 us
    psum x1, waiting for transfers between devices, shards(): lax.psum(lax.psum_scatter(expert_term, 'dev', scatter_dimension=1, tiled=...  61.2 us
  transfers between devices with their start and end apart: 5, of which 5 were waited for; matrix products, arithmetic and copies ran while one was open for 0% of the time, Pallas kernels for 0%

commit v1 on v0

--- a/solution.py
+++ b/solution.py
@@ -103,7 +103,8 @@
     slot_mask, spread = slot_layout(routes, route_weights, local_ids)
     result = expert_results(full_rows, slot_mask, w_gate, w_up, w_down)
     expert_term = jnp.einsum("ecr,ecd->rd", spread, result, precision=lax.Precision.HIGHEST)
-    mixture = lax.psum(lax.psum_scatter(expert_term, "dev", scatter_dimension=1, tiled=True), "sec")
+    inner_x = lax.psum_scatter(expert_term, "dev", scatter_dimension=1, tiled=True)
+    mixture = lax.all_gather(inner_x, "sec").sum(axis=0)
     return (hidden + mixture).astype(jnp.bfloat16)
 
 

time: 654 us -> 623 us (0.953)
  waiting for transfers between devices: 535 us -> 474 us
  blocking collectives: 68 us -> 99.4 us
    psum x1 -> x0, waiting for transfers between devices: 61.2 us -> none  [shards(): lax.psum(lax.psum_scatter(expert_term, 'dev', scatter_dimension=1, tiled=...]
    all_gather x0 -> x1, blocking collectives: none -> 31.4 us  [shards(): mixture = lax.all_gather(inner_x, 'sec').sum(axis=0)]
  transfers between devices with their start and end apart: 5 -> 4, of which waited for: 5 -> 4; matrix products, arithmetic and copies ran while one was open for 0% -> 0% of each run, Pallas kernels for 0% -> 0%
where the time goes in v1:
time: 623 us; the launch traced here: 622 us
  waiting for transfers between devices  474 us (76%)
  blocking collectives  99.4 us (16%)
  matrix products  28.3 us (5%)
  between operations  13.2 us (2%)
    reduce_scatter x1, waiting for transfers between devices, shards(): lax.psum_scatter(expert_term, 'dev', scatter_dimension=1, tiled=True)  162 us
    all_gather x1, waiting for transfers between devices, shards(): lax.all_gather(attn, 'dev', axis=0, tiled=True)  133 us
    all_gather x1, waiting for transfers between devices, shards(): full_rows = lax.all_gather(normed, 'dev', axis=1, tiled=True)  117 us
    psum x1, blocking collectives, shards(): lax.psum(jnp.sum(hidden * hidden, axis=-1, keepdims=True), 'dev')  68 us
    psum x1, waiting for transfers between devices, shards(): hidden = residual.astype(jnp.float32) + lax.psum(partial_out, 'sec')  62.2 us
    all_gather x1, blocking collectives, shards(): mixture = lax.all_gather(inner_x, 'sec').sum(axis=0)  31.4 us
  transfers between devices with their start and end apart: 4, of which 4 were waited for; matrix products, arithmetic and copies ran while one was open for 0% of the time, Pallas kernels for 0%

profile of v1, /device:TPU:1, one launch (start us, length us, event | category | flops | bytes accessed | tf_op | source)
XLA Modules:
  0.0 622.3 jit_solution(15297765289965824629)
XLA Ops:
  6.5 0.0 copy-start
  6.5 0.0 copy-start.2
  6.5 0.0 all-gather.4.cloned.1.call-start
  6.5 0.8 bitcast_convert_fusion
  7.3 0.7 iota_compare_fusion.1
  8.0 0.9 fusion.46
  8.9 0.0 copy-start.5
  8.9 0.0 copy-start.3
  8.9 0.0 copy-start.4
  8.9 2.4 select_reduce_fusion
  11.3 0.2 fusion.24
  11.6 2.1 fusion.21
  13.7 0.6 copy.34
  14.3 0.0 all-gather.4.cloned.1.call-update
  14.3 0.0 all-reduce.2.cloned.1.call-start
  14.4 132.9 %all-gather.4.cloned.1.call-done = bf16[256,2048]{1,0:T(8,128)(2,1)} async-done(((bf16[8,2048]{1,0:T(8,128)(2,1)}), bf16[256,2048]{1,0:T(8,128)(2,1)}) %all-gather.4.cloned.1.call-update) | async-done | bytes 1048592 | tf_op jit(solution)/shard_map/all_gather | solution.py:93
  147.2 0.0 copy-done
  147.2 2.3 fusion.55
  149.5 0.0 all-reduce.2.cloned.1.call-update
  149.5 0.0 all-gather.6.cloned.1.call-start
  149.6 62.2 %all-reduce.2.cloned.1.call-done = f32[256,128]{1,0:T(8,128)} async-done(((f32[256,128]{1,0:T(8,128)}), f32[256,128]{1,0:T(8,128)}) %all-reduce.2.cloned.1.call-update) | async-done | bytes 131088 | tf_op jit(solution)/shard_map/psum | solution.py:97
  211.8 0.0 copy-done.2
  211.8 1.0 multiply_reduce_fusion
  212.9 68.0 %psum.15 = f32[256,1]{0,1:T(1,128)S(1)} all-reduce(f32[256,1]{0,1:T(1,128)S(1)} %bitcast.69), channel_id=1, replica_groups=mesh['sec'=4,'dev'=32] {'dev'}, use_global_device_ids=true, to_apply=%region_8.9 | all-reduce | flops 256 | bytes 2048 | tf_op jit(solution)/shard_map/psum | solution.py:98
  280.9 0.0 copy-done.5
  280.9 1.6 multiply_convert_fusion
  282.5 0.0 all-gather.6.cloned.1.call-update
  282.6 0.0 reduce-scatter.2.cloned.1.call-start
  282.6 0.0 copy-done.3
  282.6 0.1 compare_reduce_fusion
  282.7 0.6 reduce-window.6
  283.4 0.2 slice_reduce_fusion
  283.6 0.2 reduce-window.9
  283.7 0.1 add_bitcast_fusion
  283.8 0.0 copy-done.4
  283.8 0.1 fusion.49
  283.9 116.7 %all-gather.6.cloned.1.call-done = bf16[256,4096]{1,0:T(8,128)(2,1)} async-done(((bf16[256,128]{1,0:T(8,128)(2,1)}), bf16[256,4096]{1,0:T(8,128)(2,1)}) %all-gather.6.cloned.1.call-update) | async-done | bytes 2097168 | tf_op jit(solution)/shard_map/all_gather | solution.py:100
  400.6 2.0 convolution_convert_fusion
  402.6 3.8 fusion.56
  406.4 8.1 %fusion.11 = f32[2,64,4096]{2,1,0:T(8,128)} fusion(bf16[2,384,4096]{2,1,0:T(8,128)(2,1)} %param.23, bf16[2,64,4096]{2,1,0:T(8,128)(2,1)S(1)} %convolution_convert_fusion, bf16[2,4096,384]{2,1,0:T(8,128)(2,1)} %param.22, f32[2,64,384]{2,1,0:T(8,128)S(1)} %fusion.56), kind=kOutput, calls=%fused_computation.12 | convolution fusion | flops 805601280 | bytes 15925248 | tf_op jit(solution)/shard_map/ecf,efd->ecd/dot_general | solution.py:74
  414.5 6.7 %convolution_bitcast_fusion = f32[256,4096]{1,0:T(8,128)} fusion(f32[2,64,4096]{2,1,0:T(8,128)} %fusion.11, f32[2,256]{1,0:T(2,128)S(1)} %bitcast.67, s32[2,256]{1,0:T(2,128)S(1)} %bitcast.60, pred[2,256]{1,0:T(4,128)(4,1)S(1)} %bitcast.64), kind=kOutput, calls=%fused_computation | convolution fusion | flops 1610711040 | bytes 6296064 | tf_op jit(solution)/shard_map/ecr,ecd->rd/dot_general | solution.py:105
  421.2 0.0 copy-start.1
  421.2 0.0 reduce-scatter.2.cloned.1.call-update
  421.3 162.4 %reduce-scatter.2.cloned.1.call-done = f32[256,128]{1,0:T(8,128)} async-done(((f32[256,4096]{1,0:T(8,128)}), f32[256,128]{1,0:T(8,128)}) %reduce-scatter.2.cloned.1.call-update) | async-done | bytes 131088 | tf_op jit(solution)/shard_map/reduce_scatter | solution.py:106
  583.6 31.4 %all-gather = f32[1024,128]{1,0:T(8,128)S(1)} all-gather(f32[256,128]{1,0:T(8,128)} %reduce-scatter.2.cloned.1.call-done), channel_id=2, replica_groups=mesh['sec'=4,'dev'=32] {'sec'}, dimensions={0}, use_global_device_ids=true | all-gather | bytes 655360 | tf_op jit(solution)/shard_map/all_gather | solution.py:107
  615.1 0.0 copy-done.1
  615.1 0.7 add_convert_fusion
  (8 shorter events, 0.1 us)
Async XLA Ops:
  6.5 140.7 %copy-start = (bf16[2048,128]{1,0:T(8,128)(2,1)S(1)}, bf16[2048,128]{1,0:T(8,128)(2,1)}, u32[]{:S(2)}) copy-start(bf16[2048,128]{1,0:T(8,128)(2,1)} %param.17) | copy-start | bytes 1572868
  6.5 205.3 %copy-start.2 = (bf16[256,128]{1,0:T(8,128)(2,1)S(1)}, bf16[256,128]{1,0:T(8,128)(2,1)}, u32[]{:S(2)}) copy-start(bf16[256,128]{1,0:T(8,128)(2,1)} %param.16) | copy-start | bytes 196612
  6.5 140.7 %all-gather.4.cloned.1.call-start = ((), (), s32[]{:S(2)}) async-start(), calls=%async_computation.1 | async-start | bytes 1081344 | tf_op jit(solution)/shard_map/all_gather | solution.py:93
  8.9 272.0 %copy-start.5 = (f32[128]{0:T(128)S(1)}, f32[128]{0:T(128)}, u32[]{:S(2)}) copy-start(f32[128]{0:T(128)} %param.18) | copy-start | bytes 1540
  8.9 273.7 %copy-start.3 = (s32[256,8]{0,1:T(8,128)S(1)}, s32[256,8]{0,1:T(8,128)}, u32[]{:S(2)}) copy-start(s32[256,8]{0,1:T(8,128)} %param.19) | copy-start | bytes 24580
  8.9 274.9 %copy-start.4 = (f32[256,8]{0,1:T(8,128)S(1)}, f32[256,8]{0,1:T(8,128)}, u32[]{:S(2)}) copy-start(f32[256,8]{0,1:T(8,128)} %param.20) | copy-start | bytes 24580
  14.3 197.5 %all-reduce.2.cloned.1.call-start = ((), (), s32[]{:S(2)}) async-start(), calls=%async_computation.2 | async-start | bytes 262144 | tf_op jit(solution)/shard_map/psum | solution.py:97
  149.5 251.0 %all-gather.6.cloned.1.call-start = ((), (), s32[]{:S(2)}) async-start(), calls=%async_computation.3 | async-start | bytes 2162688 | tf_op jit(solution)/shard_map/all_gather | solution.py:100
  282.6 301.1 %reduce-scatter.2.cloned.1.call-start = ((), (), s32[]{:S(2)}) async-start(), calls=%async_computation.4 | async-start | bytes 4325376 | tf_op jit(solution)/shard_map/reduce_scatter | solution.py:106
  421.2 193.8 %copy-start.1 = (f32[256,128]{1,0:T(8,128)S(1)}, f32[256,128]{1,0:T(8,128)}, u32[]{:S(2)}) copy-start(f32[256,128]{1,0:T(8,128)} %all-reduce.2.cloned.1.call-done) | copy-start | bytes 393220
Sparse Core Ops, SparseCore 0:
  14.4 132.7 all-gather.3
  149.7 62.0 all-reduce.1
  282.7 117.8 all-gather.5
  421.4 162.2 reduce-scatter.1
